TPU v7x, 512 devices: a whole 4x8x8 slice. The times are simulated.
512 devices in a mesh: dom: 64 (over x, y, z_lo), col: 8 (over z_hi, core).
Axes of the slice: x: 4, y: 8, z: 8 (z_hi: 4, z_lo: 2; z = z_hi * 2 + z_lo), core: 2. Of those that a mesh axis runs over, the one named last changes fastest.
Arguments:
- inverse: bfloat16 [64, 1664, 1664], P('dom', 'col'), may hold values from -1 to 4, as said below
- trace_map: bfloat16 [64, 512, 1664], P('dom', 'col'), may hold values from -0.15625 to 0.15625
- panel_coupling: bfloat16 [64, 1664, 128], P('dom'), may hold values from -6 to 6
- coupling: float32 [64, 6, 1664], P('dom', None, 'col'), may hold values from 0.15 to 0.9
- neighbours: int32 [64, 6], P('dom'), may hold values from 0 to 63, as said below
- iface_count: int32 [64], replicated, may hold values from 26 to 104, as said below
- surface_rows: int32 [64, 8, 1, 64], P('dom', 'col'), may hold values from 0 to 63
- factor: float32 [32768, 2048], P(('dom', 'col')), may hold values from -2 to 2
- colloc: float32 [3, 32768], P(None, ('dom', 'col')), may hold values from -1 to 1
- quad_points: float32 [3, 4, 32768], P(None, None, ('dom', 'col')), may hold values from -1 to 1
- quad_weight: float32 [4, 32768], P(None, ('dom', 'col')), may hold values from 2 to 16
- panel_block: int32 [2], replicated, may hold values from 0 to 511
Outputs:
- panel_columns: float32 [32768, 128], P(('dom', 'col'))
Inputs may be any that keep to these rules, and one draw needn't show every extreme that they name: Each domain's inverse is symmetric. `neighbours`: each domain lists 6 different domains, never itself. `iface_count`: some domain has exactly 104.
All inputs are finite; a program needn't handle non-finite values.
Results may differ from a plain program's by a relative error of at most 0.007.
Values may be sent and summed in bfloat16 or wider, within the bound.
No kernel may reach another device: no remote copies, remote signals or barrier semaphores. Data moves between devices by JAX's collectives and lax.ppermute only.
A program may use at most 64 MiB of HBM per device.

v0:
```python
import math
import jax
import jax.numpy as jnp
from jax import lax
from jax.sharding import PartitionSpec as P

MB = 208
P_SIZE = 64
NPAN = 2
SLOTS = 1
WAVE_NUMBER = 8.0
SMOOTHING = 0.05


def broadcast(block, axis, source):
    block = jnp.where(lax.axis_index(axis) == source, block, jnp.zeros_like(block))
    return lax.psum(block, axis)


def local(
    inverse,
    trace_map,
    panel_coupling,
    coupling,
    neighbours,
    iface_count,
    surface_rows,
    factor,
    colloc,
    quad_points,
    quad_weight,
    panel_block,
):
    dom_index = lax.axis_index("dom")
    col_index = lax.axis_index("col")
    domain_count = lax.axis_size("dom")
    inverse_rows = inverse[0]
    block_rows = inverse_rows.shape[0]
    panel_loads = panel_coupling[0]
    column_count = panel_loads.shape[1]
    first_row = col_index * block_rows
    own_loads = lax.dynamic_slice_in_dim(panel_loads, first_row, block_rows, 0)
    row_numbers = first_row + jnp.arange(block_rows, dtype=jnp.int32)
    own_count = iface_count[dom_index]
    live_rows = (row_numbers % MB < own_count).astype(jnp.float32)[:, None]
    first_apply = jnp.dot(inverse_rows, panel_loads, preferred_element_type=jnp.float32)
    first_values = (first_apply * live_rows).astype(jnp.bfloat16)
    weights_here = coupling[0]
    listed = neighbours[0]
    shards = lax.all_gather(first_values[None], "dom", axis=0, tiled=True)
    count_here = shards.shape[0]
    matches = (listed[:, None] == jnp.arange(count_here, dtype=jnp.int32)[None, :]).astype(
        jnp.float32
    )
    factors = jnp.einsum("ke,kr->er", matches, weights_here)
    correction = jnp.sum(factors[:, :, None] * shards, axis=0)
    loaded = (own_loads.astype(jnp.float32) - live_rows * correction).astype(jnp.bfloat16)
    map_rows = trace_map[0]
    columns = inverse_rows
    second_rows = jnp.dot(
        columns,
        lax.all_gather(loaded, "col", axis=0, tiled=True),
        preferred_element_type=jnp.float32,
    ).astype(jnp.bfloat16)
    columns = map_rows
    traces = jnp.dot(
        columns,
        lax.all_gather(second_rows, "col", axis=0, tiled=True),
        preferred_element_type=jnp.float32,
    )
    traces = traces.astype(jnp.bfloat16).reshape(SLOTS, domain_count, column_count)
    arrived = lax.all_to_all(traces, "dom", split_axis=1, concat_axis=1, tiled=True)
    row_slots = surface_rows[0, 0].reshape(-1)
    factor_rows = factor.shape[0]
    surface_sum = (
        jnp.zeros((factor_rows, column_count), jnp.float32)
        .at[row_slots]
        .add(arrived.reshape(-1, column_count).astype(jnp.float32))
    )
    factor_list = []
    points_list = []
    weights_list = []
    for panel_number in range(NPAN):
        begin_row = panel_block[panel_number] * P_SIZE
        owner_device = begin_row // factor_rows
        received = (
            broadcast(factor, ("dom", "col"), owner_device),
            broadcast(quad_points, ("dom", "col"), owner_device),
            broadcast(quad_weight, ("dom", "col"), owner_device),
        )
        factor_list.append(received[0])
        points_list.append(received[1])
        weights_list.append(received[2])
    panel_factor = jnp.concatenate(factor_list, axis=0)
    panel_points = jnp.concatenate(points_list, axis=2)
    panel_weights = jnp.concatenate(weights_list, axis=1)
    shifted = colloc[:, :, None, None] - panel_points[:, None, :, :]
    squared = jnp.sum(shifted * shifted, axis=0)
    green_values = jnp.cos(WAVE_NUMBER * jnp.sqrt(squared)) / (
        4.0 * math.pi * jnp.sqrt(squared + SMOOTHING * SMOOTHING)
    )
    kernel_block = jnp.sum(panel_weights[None, :, :] * green_values, axis=1)
    prior_update = lax.dot_general(
        factor,
        panel_factor,
        (((1,), (1,)), ((), ())),
        precision=lax.Precision.HIGHEST,
        preferred_element_type=jnp.float32,
    )
    return kernel_block - surface_sum - prior_update


def solution(mesh):
    in_specs = (
        P("dom", "col", None),
        P("dom", "col", None),
        P("dom", None, None),
        P("dom", None, "col"),
        P("dom", None),
        P(),
        P("dom", "col", None, None),
        P(("dom", "col"), None),
        P(None, ("dom", "col")),
        P(None, None, ("dom", "col")),
        P(None, ("dom", "col")),
        P(),
    )
    out_specs = P(("dom", "col"), None)
    return jax.shard_map(local, mesh=mesh, in_specs=in_specs, out_specs=out_specs, check_vma=False)
```

profile of v0, /device:TPU:1, one launch (start us, length us, event | category | flops | bytes accessed | tf_op | source)
XLA Modules:
  0.0 388.6 jit_solution(3497062849710801463)
XLA Ops:
  7.4 0.0 all-gather.3.cloned.1.call-start
  7.5 1.3 dynamic_slice.7
  8.7 0.7 compare_convert_fusion
  9.4 2.0 fusion.1
  11.4 0.0 all-gather.3.cloned.1.call-update
  11.4 0.0 all-reduce.4.cloned.1.call-start
  11.5 1.3 fusion.24
  14.1 2.1 broadcast_select_fusion.1
  16.3 0.0 all-reduce.4.cloned.1.call-update
  16.3 0.0 copy-done.6
  16.3 0.0 copy-done.3
  16.4 108.0 %all-reduce = (f32[3,4,64]{2,1,0:T(4,128)S(1)}, f32[3,4,64]{2,1,0:T(4,128)S(1)}, f32[4,64]{1,0:T(4,128)S(1)}, f32[4,64]{1,0:T(4,128)S(1)}) all-reduce(f32[3,4,64]{2,1,0:T(4,128)S(1)} %get-tuple-element.14, f32[3,4,64]{2,1,0:T(4,128)S(1)} %get-tuple-element.13, ...), channel_id=1, replica_groups=mesh['dom'=64,'col'=8] {'dom','col'}, use_global_device_ids=true, to_apply=%region_3.4 | all-reduce | flops 2048 | bytes 16384 | tf_op jit(solution)/shard_map/psum | solution.py:17
  124.3 0.1 pad_maximum_fusion
  124.4 0.1 pad_maximum_fusion.1
  124.5 0.0 copy-done.4
  124.5 0.3 fusion.18
  124.8 0.0 copy-done.5
  124.8 0.1 multiply_reduce_fusion
  124.9 149.1 %all-gather.3.cloned.1.call-done = bf16[13312,128]{1,0:T(8,128)(2,1)} async-done(((bf16[208,128]{1,0:T(8,128)(2,1)}), bf16[13312,128]{1,0:T(8,128)(2,1)}) %all-gather.3.cloned.1.call-update) | async-done | bytes 3407888 | tf_op jit(solution)/shard_map/all_gather | solution.py:50
  274.0 4.0 %fusion = f32[208,128]{1,0:T(8,128)S(1)} fusion(bf16[64,208,128]{2,1,0:T(8,128)(2,1)} %bitcast.46, f32[64,208]{1,0:T(8,128)S(1)} %fusion.18), kind=kLoop, calls=%fused_computation.2 | loop fusion | flops 5085184 | bytes 3567616 | tf_op jit(solution)/shard_map/reduce_sum | solution.py:56
  278.1 0.9 fusion.12
  279.0 66.1 %all_gather.10 = bf16[1664,128]{1,0:T(8,128)(2,1)S(1)} all-gather(bf16[208,128]{1,0:T(8,128)(2,1)S(1)} %fusion.12), channel_id=1, replica_groups=mesh['dom'=64,'col'=8] {'col'}, dimensions={0}, use_global_device_ids=true | all-gather | bytes 479232 | tf_op jit(solution)/shard_map/all_gather | solution.py:62
  345.1 0.4 fusion.2
  345.4 14.9 %all_gather.11 = bf16[1664,128]{1,0:T(8,128)(2,1)S(1)} all-gather(bf16[208,128]{1,0:T(8,128)(2,1)S(1)} %fusion.2), channel_id=1, replica_groups=mesh['dom'=64,'col'=8] {'col'}, dimensions={0}, use_global_device_ids=true | all-gather | bytes 479232 | tf_op jit(solution)/shard_map/all_gather | solution.py:68
  360.4 0.2 fusion.4
  360.6 0.6 copy.15
  361.2 6.8 %all-to-all-start = ((bf16[1,64,128]{2,0,1:T(2,128)(2,1)}), bf16[1,64,128]{2,0,1:T(2,128)(2,1)S(1)}, u32[]{:S(2)}, u32[]{:S(2)}) async-start(bf16[1,64,128]{2,0,1:T(2,128)(2,1)} %copy.15), calls=%async_computation | async-start | bytes 65536 | tf_op jit(solution)/shard_map/all_to_all | solution.py:72
  368.0 0.5 multiply_reduce_fusion.1
  368.6 8.7 %all-to-all-done = bf16[1,64,128]{2,0,1:T(2,128)(2,1)S(1)} async-done(((bf16[1,64,128]{2,0,1:T(2,128)(2,1)}), bf16[1,64,128]{2,0,1:T(2,128)(2,1)S(1)}, u32[]{:S(2)}, u32[]{:S(2)}) %all-to-all-start) | async-done | bytes 16416 | tf_op jit(solution)/shard_map/all_to_all | solution.py:72
  377.2 0.8 scatter_custom_fusion
  378.1 0.0 all-reduce.4.cloned.1.call-done
  378.1 3.0 fusion.3
  (17 shorter events, 0.0 us)
Async XLA Ops:
  7.4 2.0 copy-start
  7.4 8.9 %copy-start.8 = (s32[1,1,1,64]{3,2,1,0:T(1,128)S(1)}, s32[1,1,1,64]{3,2,1,0:T(1,128)}, u32[]{:S(2)}) copy-start(s32[1,1,1,64]{3,2,1,0:T(1,128)} %param.18) | copy-start | bytes 772
  7.4 9.0 %copy-start.6 = (f32[4,64]{1,0:T(4,128)S(1)}, f32[4,64]{1,0:T(4,128)}, u32[]{:S(2)}) copy-start(f32[4,64]{1,0:T(4,128)} %param.22) | copy-start | bytes 3076
  7.4 9.0 %copy-start.3 = (f32[3,4,64]{2,1,0:T(4,128)S(1)}, f32[3,4,64]{2,1,0:T(4,128)}, u32[]{:S(2)}) copy-start(f32[3,4,64]{2,1,0:T(4,128)} %param.21) | copy-start | bytes 9220
  7.4 117.1 %copy-start.7 = (s32[1,6]{1,0:T(1,128)S(1)}, s32[1,6]{1,0:T(1,128)}, u32[]{:S(2)}) copy-start(s32[1,6]{1,0:T(1,128)} %param.16) | copy-start | bytes 76
  7.4 117.1 %copy-start.4 = (f32[1,6,208]{2,0,1:T(1,128)S(1)}, f32[1,6,208]{2,0,1:T(1,128)}, u32[]{:S(2)}) copy-start(f32[1,6,208]{2,0,1:T(1,128)} %param.15) | copy-start | bytes 14980
  7.4 117.4 %copy-start.5 = (f32[3,64]{1,0:T(4,128)S(1)}, f32[3,64]{1,0:T(4,128)}, u32[]{:S(2)}) copy-start(f32[3,64]{1,0:T(4,128)} %param.20) | copy-start | bytes 2308
  7.4 266.6 %all-gather.3.cloned.1.call-start = ((), (), s32[]{:S(2)}) async-start(), calls=%async_computation.1 | async-start | bytes 3461120 | tf_op jit(solution)/shard_map/all_gather | solution.py:50
  11.4 366.7 %all-reduce.4.cloned.1.call-start = ((), (), s32[]{:S(2)}) async-start(), calls=%async_computation.2 | async-start | bytes 2097152 | tf_op jit(solution)/shard_map/psum | solution.py:17
  16.3 344.1 %copy-start.2 = (bf16[1,64,1664]{2,1,0:T(8,128)(2,1)S(1)}, bf16[1,64,1664]{2,1,0:T(8,128)(2,1)}, u32[]{:S(2)}) copy-start(bf16[1,64,1664]{2,1,0:T(8,128)(2,1)} %param.13) | copy-start | bytes 638980
  274.0 104.1 %copy-start.1 = (f32[64,2048]{1,0:T(8,128)S(1)}, f32[64,2048]{1,0:T(8,128)}, u32[]{:S(2)}) copy-start(f32[64,2048]{1,0:T(8,128)} %param.19) | copy-start | bytes 1572868
  361.2 16.0 %all-to-all-start = ((bf16[1,64,128]{2,0,1:T(2,128)(2,1)}), bf16[1,64,128]{2,0,1:T(2,128)(2,1)S(1)}, u32[]{:S(2)}, u32[]{:S(2)}) async-start(bf16[1,64,128]{2,0,1:T(2,128)(2,1)} %copy.15), calls=%async_computation | async-start | bytes 65536 | tf_op jit(solution)/shard_map/all_to_all | solution.py:72
Sparse Core Ops, SparseCore 0:
  11.6 262.4 all-gather.2
Sparse Core Ops, SparseCore 1:
  17.2 283.3 all-reduce.3
where the time goes:
time: 389 us
  blocking collectives  189 us (49%)
  waiting for transfers between devices  158 us (41%)
  between operations  16.3 us (4%)
  other arithmetic  9.37 us (2%)
  starting transfers between devices  6.86 us (2%)
  matrix products  5.84 us (2%)
    all_gather x1, waiting for transfers between devices, local(): shards = lax.all_gather(first_values[None], 'dom', axis=0, tiled=True)  149 us
    psum x1, blocking collectives, broadcast(): return lax.psum(block, axis)  108 us
    all_gather x1, blocking collectives, local(): lax.all_gather(loaded, 'col', axis=0, tiled=True)  66.1 us
    all_gather x1, blocking collectives, local(): lax.all_gather(second_rows, 'col', axis=0, tiled=True)  14.9 us
    all_to_all x1, waiting for transfers between devices, local(): lax.all_to_all(traces, 'dom', split_axis=1, concat_axis=1, tiled=True)  8.67 us
  transfers between devices with their start and end apart: 3, of which 2 were waited for; matrix products, arithmetic and copies ran while one was open for 3% of the time, Pallas kernels for 0%

commit v1 on v0

--- a/solution.py
+++ b/solution.py
@@ -10,6 +10,13 @@
 SLOTS = 1
 WAVE_NUMBER = 8.0
 SMOOTHING = 0.05
+
+
+def all_by_exchange(x, name, dim):
+    peers = lax.axis_size(name)
+    parts = jnp.stack([x for _ in range(peers)])
+    parts = lax.all_to_all(parts, name, split_axis=0, concat_axis=0)
+    return jnp.concatenate(parts, axis=dim)
 
 
 def broadcast(block, axis, source):
@@ -58,9 +65,7 @@
     map_rows = trace_map[0]
     columns = inverse_rows
     second_rows = jnp.dot(
-        columns,
-        lax.all_gather(loaded, "col", axis=0, tiled=True),
-        preferred_element_type=jnp.float32,
+        columns, all_by_exchange(loaded, "col", 0), preferred_element_type=jnp.float32
     ).astype(jnp.bfloat16)
     columns = map_rows
     traces = jnp.dot(

time: 389 us -> 480 us (1.23)
  waiting for transfers between devices: 158 us -> 266 us
  blocking collectives: 189 us -> 116 us
  starting transfers between devices: 6.86 us -> 61.5 us
    all_gather x1, waiting for transfers between devices: 149 us -> 257 us  [local(): shards = lax.all_gather(first_values[None], 'dom', axis=0, tiled=True)]
    all_gather x1 -> x0, blocking collectives: 66.1 us -> none  [local(): lax.all_gather(loaded, 'col', axis=0, tiled=True)]
    all_to_all x0 -> x1, starting transfers between devices: none -> 55 us  [all_by_exchange(): parts = lax.all_to_all(parts, name, split_axis=0, concat_axis=0)]
    psum x1, blocking collectives: 108 us -> 100 us  [broadcast(): return lax.psum(block, axis)]
  transfers between devices with their start and end apart: 3 -> 4, of which waited for: 2 -> 2; matrix products, arithmetic and copies ran while one was open for 3% -> 3% of each run, Pallas kernels for 0% -> 0%
where the time goes in v1:
time: 480 us; the launch traced here: 479 us
  waiting for transfers between devices  266 us (55%)
  blocking collectives  116 us (24%)
  starting transfers between devices  61.5 us (13%)
  between operations  16.3 us (3%)
  other arithmetic  9.39 us (2%)
  matrix products  5.83 us (1%)
    all_gather x1, waiting for transfers between devices, local(): shards = lax.all_gather(first_values[None], 'dom', axis=0, tiled=True)  257 us
    psum x1, blocking collectives, broadcast(): return lax.psum(block, axis)  100 us
    all_to_all x1, starting transfers between devices, all_by_exchange(): parts = lax.all_to_all(parts, name, split_axis=0, concat_axis=0)  55 us
    all_gather x1, blocking collectives, local(): lax.all_gather(second_rows, 'col', axis=0, tiled=True)  16.3 us
  transfers between devices with their start and end apart: 4, of which 2 were waited for; matrix products, arithmetic and copies ran while one was open for 3% of the time, Pallas kernels for 0%

profile of v1, /device:TPU:1, one launch (start us, length us, event | category | flops | bytes accessed | tf_op | source)
XLA Modules:
  0.0 479.5 jit_solution(17202009842234084114)
XLA Ops:
  7.4 0.0 all-gather.3.cloned.1.call-start
  7.4 1.3 dynamic_slice.7
  8.7 0.7 compare_convert_fusion
  9.4 2.0 fusion.1
  11.4 0.0 all-gather.3.cloned.1.call-update
  11.4 0.0 all-reduce.4.cloned.1.call-start
  11.4 1.3 fusion.26
  14.0 2.2 broadcast_select_fusion.1
  16.2 0.0 all-reduce.4.cloned.1.call-update
  16.2 0.0 copy-done.3
  16.2 0.3 fusion.20
  16.5 257.4 %all-gather.3.cloned.1.call-done = bf16[13312,128]{1,0:T(8,128)(2,1)} async-done(((bf16[208,128]{1,0:T(8,128)(2,1)}), bf16[13312,128]{1,0:T(8,128)(2,1)}) %all-gather.3.cloned.1.call-update) | async-done | bytes 3407888 | tf_op jit(solution)/shard_map/all_gather | solution.py:57
  273.9 4.0 fusion
  277.9 0.9 fusion.14
  278.8 0.8 stack.5
  279.7 55.0 %all-to-all-start = ((bf16[8,208,128]{2,1,0:T(8,128)(2,1)}), bf16[8,208,128]{2,1,0:T(8,128)(2,1)S(1)}, u32[]{:S(2)}, u32[]{:S(2)}) async-start(bf16[8,208,128]{2,1,0:T(8,128)(2,1)} %stack.5), calls=%async_computation | async-start | bytes 851968 | tf_op jit(solution)/shard_map/all_to_all | solution.py:18
  334.7 100.0 %all-reduce = (f32[3,4,64]{2,1,0:T(4,128)S(1)}, f32[3,4,64]{2,1,0:T(4,128)S(1)}, f32[4,64]{1,0:T(4,128)S(1)}, f32[4,64]{1,0:T(4,128)S(1)}) all-reduce(f32[3,4,64]{2,1,0:T(4,128)S(1)} %get-tuple-element.14, f32[3,4,64]{2,1,0:T(4,128)S(1)} %get-tuple-element.13, ...), channel_id=1, replica_groups=mesh['dom'=64,'col'=8] {'dom','col'}, use_global_device_ids=true, to_apply=%region_3.4 | all-reduce | flops 2048 | bytes 16384 | tf_op jit(solution)/shard_map/psum | solution.py:24
  434.7 0.1 pad_maximum_fusion.1
  434.8 0.1 pad_maximum_fusion
  434.8 0.1 multiply_reduce_fusion
  435.0 0.0 copy-done.8
  435.0 0.0 all-to-all-done
  435.0 0.4 fusion.2
  435.4 16.3 %all_gather.7 = bf16[1664,128]{1,0:T(8,128)(2,1)S(1)} all-gather(bf16[208,128]{1,0:T(8,128)(2,1)S(1)} %fusion.2), channel_id=1, replica_groups=mesh['dom'=64,'col'=8] {'col'}, dimensions={0}, use_global_device_ids=true | all-gather | bytes 479232 | tf_op jit(solution)/shard_map/all_gather | solution.py:73
  451.7 0.2 fusion.4
  451.9 0.6 copy.15
  452.5 6.4 %all-to-all-start.1 = ((bf16[1,64,128]{2,0,1:T(2,128)(2,1)}), bf16[1,64,128]{2,0,1:T(2,128)(2,1)S(1)}, u32[]{:S(2)}, u32[]{:S(2)}) async-start(bf16[1,64,128]{2,0,1:T(2,128)(2,1)} %copy.15), calls=%async_computation.1 | async-start | bytes 65536 | tf_op jit(solution)/shard_map/all_to_all | solution.py:77
  458.9 0.5 multiply_reduce_fusion.1
  459.5 8.7 %all-to-all-done.1 = bf16[1,64,128]{2,0,1:T(2,128)(2,1)S(1)} async-done(((bf16[1,64,128]{2,0,1:T(2,128)(2,1)}), bf16[1,64,128]{2,0,1:T(2,128)(2,1)S(1)}, u32[]{:S(2)}, u32[]{:S(2)}) %all-to-all-start.1) | async-done | bytes 16416 | tf_op jit(solution)/shard_map/all_to_all | solution.py:77
  468.2 0.8 scatter_custom_fusion
  469.0 0.0 all-reduce.4.cloned.1.call-done
  469.0 3.0 fusion.3
  (19 shorter events, 0.0 us)
Async XLA Ops:
  7.4 2.0 copy-start
  7.4 8.8 %copy-start.3 = (f32[3,4,64]{2,1,0:T(4,128)S(1)}, f32[3,4,64]{2,1,0:T(4,128)}, u32[]{:S(2)}) copy-start(f32[3,4,64]{2,1,0:T(4,128)} %param.21) | copy-start | bytes 9220
  7.4 8.9 %copy-start.7 = (s32[1,6]{1,0:T(1,128)S(1)}, s32[1,6]{1,0:T(1,128)}, u32[]{:S(2)}) copy-start(s32[1,6]{1,0:T(1,128)} %param.16) | copy-start | bytes 76
  7.4 8.9 %copy-start.4 = (f32[1,6,208]{2,0,1:T(1,128)S(1)}, f32[1,6,208]{2,0,1:T(1,128)}, u32[]{:S(2)}) copy-start(f32[1,6,208]{2,0,1:T(1,128)} %param.15) | copy-start | bytes 14980
  7.4 266.5 %all-gather.3.cloned.1.call-start = ((), (), s32[]{:S(2)}) async-start(), calls=%async_computation.2 | async-start | bytes 3461120 | tf_op jit(solution)/shard_map/all_gather | solution.py:57
  11.4 457.6 %all-reduce.4.cloned.1.call-start = ((), (), s32[]{:S(2)}) async-start(), calls=%async_computation.3 | async-start | bytes 2097152 | tf_op jit(solution)/shard_map/psum | solution.py:24
  16.2 318.5 %copy-start.6 = (f32[4,64]{1,0:T(4,128)S(1)}, f32[4,64]{1,0:T(4,128)}, u32[]{:S(2)}) copy-start(f32[4,64]{1,0:T(4,128)} %param.22) | copy-start | bytes 3076
  16.2 418.7 %copy-start.5 = (f32[3,64]{1,0:T(4,128)S(1)}, f32[3,64]{1,0:T(4,128)}, u32[]{:S(2)}) copy-start(f32[3,64]{1,0:T(4,128)} %param.20) | copy-start | bytes 2308
  16.2 418.8 %copy-start.8 = (s32[1,1,1,64]{3,2,1,0:T(1,128)S(1)}, s32[1,1,1,64]{3,2,1,0:T(1,128)}, u32[]{:S(2)}) copy-start(s32[1,1,1,64]{3,2,1,0:T(1,128)} %param.18) | copy-start | bytes 772
  273.9 177.8 %copy-start.2 = (bf16[1,64,1664]{2,1,0:T(8,128)(2,1)S(1)}, bf16[1,64,1664]{2,1,0:T(8,128)(2,1)}, u32[]{:S(2)}) copy-start(bf16[1,64,1664]{2,1,0:T(8,128)(2,1)} %param.13) | copy-start | bytes 638980
  273.9 195.1 %copy-start.1 = (f32[64,2048]{1,0:T(8,128)S(1)}, f32[64,2048]{1,0:T(8,128)}, u32[]{:S(2)}) copy-start(f32[64,2048]{1,0:T(8,128)} %param.19) | copy-start | bytes 1572868
  279.7 155.3 %all-to-all-start = ((bf16[8,208,128]{2,1,0:T(8,128)(2,1)}), bf16[8,208,128]{2,1,0:T(8,128)(2,1)S(1)}, u32[]{:S(2)}, u32[]{:S(2)}) async-start(bf16[8,208,128]{2,1,0:T(8,128)(2,1)} %stack.5), calls=%async_computation | async-start | bytes 851968 | tf_op jit(solution)/shard_map/all_to_all | solution.py:18
  452.5 15.6 %all-to-all-start.1 = ((bf16[1,64,128]{2,0,1:T(2,128)(2,1)}), bf16[1,64,128]{2,0,1:T(2,128)(2,1)S(1)}, u32[]{:S(2)}, u32[]{:S(2)}) async-start(bf16[1,64,128]{2,0,1:T(2,128)(2,1)} %copy.15), calls=%async_computation.1 | async-start | bytes 65536 | tf_op jit(solution)/shard_map/all_to_all | solution.py:77
Sparse Core Ops, SparseCore 0:
  11.5 262.3 all-gather.2
Sparse Core Ops, SparseCore 1:
  17.1 283.1 all-reduce.3
